TPU v7x, 32 devices: a whole 2x2x4 slice. The times are simulated.
32 devices in a mesh: gx: 8 (over y, x, core), gy: 4 (over z).
Axes of the slice: x: 2, y: 2, z: 4, core: 2. Of those that a mesh axis runs over, the one named last changes fastest.
Arguments:
- probe_signs: int32 [32, 16, 64, 128], P(None, 'gx', 'gy'), may hold values from 0 to 1
- diagonal: float32 [16, 64, 128], P('gx', 'gy'), may hold values from 0.25 to 4
Outputs:
- diagonal_blocks: float32 [3, 32, 32], replicated
- offdiag_blocks: float32 [3, 32, 32], replicated
- next_block: float32 [32, 16, 64, 128], P(None, 'gx', 'gy')
All inputs are finite; a program needn't handle non-finite values.
Results may differ from a plain program's by a relative error of at most 0.0006.
Values sent between devices are 32-bit elements; how exact they have to be, the bound alone decides.
A program may use at most 64 MiB of HBM per device.

v0:
```python
import jax
import jax.numpy as jnp
from jax import lax
from jax.sharding import PartitionSpec as P

ITERS = 3


def with_halo(block, sides, width):
    for axis, dim in sides:
        count = lax.axis_size(axis)
        forward = [(i, i + 1) for i in range(count - 1)]
        forward.append((count - 1, 0))
        backward = [(target, source) for source, target in forward]
        low = lax.ppermute(
            lax.slice_in_dim(block, block.shape[dim] - width, None, axis=dim), axis, forward
        )
        high = lax.ppermute(lax.slice_in_dim(block, 0, width, axis=dim), axis, backward)
        block = jnp.concatenate([low, block, high], axis=dim)
    return block


def stencil(vectors, diagonal):
    padded = with_halo(vectors, (("gx", 1), ("gy", 2)), 1)
    beside = padded[:, 2:, 1:-1] + padded[:, :-2, 1:-1] + padded[:, 1:-1, 2:] + padded[:, 1:-1, :-2]
    beside = beside + jnp.roll(vectors, 1, 3) + jnp.roll(vectors, -1, 3)
    return (6.0 + diagonal)[None] * vectors - beside


def inner_block(left, right):
    return jnp.einsum("pxyz,qxyz->pq", left, right, precision=lax.Precision.HIGHEST)


def combine(vectors, matrix):
    return jnp.einsum("pxyz,pq->qxyz", vectors, matrix, precision=lax.Precision.HIGHEST)


def small_product(left, right):
    return jnp.dot(left, right, precision=lax.Precision.HIGHEST)


def inverse_lower(gram_matrix):
    lower_factor = jnp.linalg.cholesky(gram_matrix)
    identity_matrix = jnp.eye(gram_matrix.shape[0], dtype=gram_matrix.dtype)
    inverse = lax.linalg.triangular_solve(lower_factor, identity_matrix, left_side=True, lower=True)
    return (lower_factor, inverse)


def per_device(probe_signs, diagonal):
    total_cells = (
        probe_signs.shape[1]
        * lax.axis_size("gx")
        * probe_signs.shape[2]
        * lax.axis_size("gy")
        * probe_signs.shape[3]
    )
    scale_factor = 1.0 / jnp.sqrt(jnp.float32(total_cells))
    probes = (2.0 * probe_signs.astype(jnp.float32) - 1.0) * scale_factor
    probe_matrix = lax.psum(inner_block(probes, probes), ("gx", "gy"))
    lower_factor, inverse = inverse_lower(probe_matrix)
    current = combine(probes, inverse.T)
    previous = None
    coupling = None
    alphas = []
    betas = []
    for iteration in range(ITERS):
        image = stencil(current, diagonal)
        if previous is not None:
            image = image - combine(previous, coupling)
        projected, image_gram = lax.psum(
            (inner_block(current, image), inner_block(image, image)), ("gx", "gy")
        )
        remain = image - combine(current, projected)
        remain_gram = image_gram - small_product(projected.T, projected)
        lower_factor, inverse = inverse_lower(remain_gram)
        alphas.append(projected)
        betas.append(lower_factor.T)
        previous = current
        coupling = lower_factor
        current = combine(remain, inverse.T)
    return (jnp.stack(alphas), jnp.stack(betas), current)


def solution(mesh):
    in_specs = (P(None, "gx", "gy", None), P("gx", "gy", None))
    out_specs = (P(), P(), P(None, "gx", "gy", None))
    return jax.shard_map(
        per_device, mesh=mesh, in_specs=in_specs, out_specs=out_specs, check_vma=False
    )
```

profile of v0, /device:TPU:14, one launch (start us, length us, event | category | flops | bytes accessed | tf_op | source)
XLA Modules:
  0.0 253.6 jit_solution(12887706050572880338)
XLA Ops:
  2.6 40.3 %psum.49 = f32[32,32]{0,1:T(8,128)S(1)} all-reduce(f32[32,32]{0,1:T(8,128)S(1)} %convolution_bitcast_fusion.10), channel_id=1, replica_groups=mesh['gx'=8,'gy'=4] {'gx','gy'}, use_global_device_ids=true, to_apply=%region_0.0 | all-reduce | flops 1024 | bytes 8192 | tf_op jit(solution)/shard_map/psum | solution.py:59
  43.0 2.9 %cholesky.74 = f32[32,32]{1,0:T(8,128)S(1)} custom-call(f32[32,32]{1,0:T(8,128)S(1)} %fusion.38), custom_call_target="Cholesky" | custom-call | tf_op jit(solution)/shard_map/jit(cholesky)/cholesky | solution.py:43
  47.3 2.4 custom-call.8
  50.9 1.7 collective-permute-start
  53.1 3.7 %collective-permute-done.1 = f32[32,1,16,128]{3,0,2,1:T(8,128)S(1)} collective-permute-done((f32[32,1,16,128]{3,0,2,1:T(8,128)S(1)}, f32[32,1,16,128]{3,0,2,1:T(8,128)S(1)}, u32[]{:S(2)}, u32[]{:S(2)}) %collective-permute-start.1) | collective-permute-done | bytes 262176 | tf_op jit(solution)/shard_map/ppermute | solution.py:15
  59.8 2.2 collective-permute-done.2
  65.0 44.6 %all-reduce.2 = (f32[32,32]{0,1:T(8,128)S(1)}, f32[32,32]{1,0:T(8,128)S(1)}) all-reduce(f32[32,32]{0,1:T(8,128)S(1)} %convolution_bitcast_fusion.7, f32[32,32]{1,0:T(8,128)S(1)} %convolution_bitcast_fusion.8), channel_id=1, replica_groups=mesh['gx'=8,'gy'=4] {'gx','gy'}, use_global_device_ids=true, to_apply=%region_4.7 | all-reduce | flops 2048 | bytes 16384 | tf_op jit(solution)/shard_map/psum | solution.py:70
  110.5 2.9 %cholesky.85 = f32[32,32]{1,0:T(8,128)S(1)} custom-call(f32[32,32]{1,0:T(8,128)S(1)} %fusion.36), custom_call_target="Cholesky" | custom-call | tf_op jit(solution)/shard_map/jit(cholesky)/cholesky | solution.py:43
  114.8 2.4 custom-call.9
  118.2 1.7 collective-permute-start.4
  120.1 5.4 %collective-permute-done.5 = f32[32,1,16,128]{3,0,2,1:T(8,128)S(1)} collective-permute-done((f32[32,1,16,128]{3,0,2,1:T(8,128)S(1)}, f32[32,1,16,128]{3,0,2,1:T(8,128)S(1)}, u32[]{:S(2)}, u32[]{:S(2)}) %collective-permute-start.5) | collective-permute-done | bytes 262176 | tf_op jit(solution)/shard_map/ppermute | solution.py:15
  125.6 2.0 collective-permute-start.7
  127.8 2.2 collective-permute-done.6
  130.9 1.6 convolution_subtract_fusion.3
  133.6 42.3 %all-reduce.1 = (f32[32,32]{0,1:T(8,128)S(1)}, f32[32,32]{1,0:T(8,128)S(1)}) all-reduce(f32[32,32]{0,1:T(8,128)S(1)} %convolution_bitcast_fusion.4, f32[32,32]{1,0:T(8,128)S(1)} %convolution_bitcast_fusion.5), channel_id=1, replica_groups=mesh['gx'=8,'gy'=4] {'gx','gy'}, use_global_device_ids=true, to_apply=%region_6.9 | all-reduce | flops 2048 | bytes 16384 | tf_op jit(solution)/shard_map/psum | solution.py:70
  176.8 2.9 %cholesky.96 = f32[32,32]{1,0:T(8,128)S(1)} custom-call(f32[32,32]{1,0:T(8,128)S(1)} %fusion.33), custom_call_target="Cholesky" | custom-call | tf_op jit(solution)/shard_map/jit(cholesky)/cholesky | solution.py:43
  181.1 2.4 custom-call.10
  184.4 1.7 collective-permute-start.8
  186.4 4.8 %collective-permute-done.9 = f32[32,1,16,128]{3,0,2,1:T(8,128)S(1)} collective-permute-done((f32[32,1,16,128]{3,0,2,1:T(8,128)S(1)}, f32[32,1,16,128]{3,0,2,1:T(8,128)S(1)}, u32[]{:S(2)}, u32[]{:S(2)}) %collective-permute-start.9) | collective-permute-done | bytes 262176 | tf_op jit(solution)/shard_map/ppermute | solution.py:15
  191.3 2.0 collective-permute-start.11
  193.5 2.0 collective-permute-done.10
  198.7 44.0 %all-reduce = (f32[32,32]{1,0:T(8,128)S(1)}, f32[32,32]{0,1:T(8,128)S(1)}) all-reduce(f32[32,32]{1,0:T(8,128)S(1)} %convolution_bitcast_fusion.2, f32[32,32]{0,1:T(8,128)S(1)} %convolution_bitcast_fusion.1), channel_id=1, replica_groups=mesh['gx'=8,'gy'=4] {'gx','gy'}, use_global_device_ids=true, to_apply=%region_7.10 | all-reduce | flops 2048 | bytes 16384 | tf_op jit(solution)/shard_map/psum | solution.py:70
  243.6 2.9 %cholesky.107 = f32[32,32]{1,0:T(8,128)S(1)} custom-call(f32[32,32]{1,0:T(8,128)S(1)} %fusion.30), custom_call_target="Cholesky" | custom-call | tf_op jit(solution)/shard_map/jit(cholesky)/cholesky | solution.py:43
  247.9 2.4 custom-call.11
  (76 shorter events, 28.6 us)
Async XLA Ops:
  50.9 6.0 %collective-permute-start.1 = (f32[32,1,16,128]{3,0,2,1:T(8,128)S(1)}, f32[32,1,16,128]{3,0,2,1:T(8,128)S(1)}, u32[]{:S(2)}, u32[]{:S(2)}) collective-permute-start(f32[32,1,16,128]{3,0,2,1:T(8,128)S(1)} %get-tuple-element.36), channel_id=1, source_target_pairs={{0,4},{4,8},{8,12},{12,16},{16,20},{20,24},{24,28},{28,0},{1,5},{5... | collective-permute-start | bytes 786440 | tf_op jit(solution)/shard_map/ppermute | solution.py:15
  50.9 6.8 %collective-permute-start = (f32[32,1,16,128]{3,0,2,1:T(8,128)S(1)}, f32[32,1,16,128]{3,0,2,1:T(8,128)S(1)}, u32[]{:S(2)}, u32[]{:S(2)}) collective-permute-start(f32[32,1,16,128]{3,0,2,1:T(8,128)S(1)} %get-tuple-element.37), channel_id=1, source_target_pairs={{4,0},{8,4},{12,8},{16,12},{20,16},{24,20},{28,24},{0,28},{5,1},{9... | collective-permute-start | bytes 786440 | tf_op jit(solution)/shard_map/ppermute | solution.py:18
  53.1 6.7 %copy-start = (f32[2,16,128]{2,1,0:T(8,128)S(1)}, f32[2,16,128]{2,1,0:T(8,128)}, u32[]{:S(2)}) copy-start(f32[2,16,128]{2,1,0:T(8,128)} %param.6) | copy-start | bytes 49156
  57.7 4.3 %collective-permute-start.2 = (f32[32,4,1,128]{3,0,2,1:T(8,128)S(1)}, f32[32,4,1,128]{3,0,2,1:T(8,128)S(1)}, u32[]{:S(2)}, u32[]{:S(2)}) collective-permute-start(f32[32,4,1,128]{3,0,2,1:T(8,128)S(1)} %get-tuple-element.18), channel_id=1, source_target_pairs={{1,0},{2,1},{3,2},{0,3},{5,4},{6,5},{7,6},{4,7},{9,8},{10,9},{11,1... | collective-permute-start | bytes 196616 | tf_op jit(solution)/shard_map/ppermute | solution.py:18
  58.3 5.1 %collective-permute-start.3 = (f32[32,4,1,128]{3,0,2,1:T(8,128)S(1)}, f32[32,4,1,128]{3,0,2,1:T(8,128)S(1)}, u32[]{:S(2)}, u32[]{:S(2)}) collective-permute-start(f32[32,4,1,128]{3,0,2,1:T(8,128)S(1)} %get-tuple-element.19), channel_id=1, source_target_pairs={{0,1},{1,2},{2,3},{3,0},{4,5},{5,6},{6,7},{7,4},{8,9},{9,10},{10,1... | collective-permute-start | bytes 196616 | tf_op jit(solution)/shard_map/ppermute | solution.py:15
  118.1 7.4 %collective-permute-start.5 = (f32[32,1,16,128]{3,0,2,1:T(8,128)S(1)}, f32[32,1,16,128]{3,0,2,1:T(8,128)S(1)}, u32[]{:S(2)}, u32[]{:S(2)}) collective-permute-start(f32[32,1,16,128]{3,0,2,1:T(8,128)S(1)} %get-tuple-element.30), channel_id=1, source_target_pairs={{0,4},{4,8},{8,12},{12,16},{16,20},{20,24},{24,28},{28,0},{1,5},{5... | collective-permute-start | bytes 786440 | tf_op jit(solution)/shard_map/ppermute | solution.py:15
  118.2 7.4 %collective-permute-start.4 = (f32[32,1,16,128]{3,0,2,1:T(8,128)S(1)}, f32[32,1,16,128]{3,0,2,1:T(8,128)S(1)}, u32[]{:S(2)}, u32[]{:S(2)}) collective-permute-start(f32[32,1,16,128]{3,0,2,1:T(8,128)S(1)} %get-tuple-element.31), channel_id=1, source_target_pairs={{4,0},{8,4},{12,8},{16,12},{20,16},{24,20},{28,24},{0,28},{5,1},{9... | collective-permute-start | bytes 786440 | tf_op jit(solution)/shard_map/ppermute | solution.py:18
  125.5 4.5 %collective-permute-start.6 = (f32[32,4,1,128]{3,0,2,1:T(8,128)S(1)}, f32[32,4,1,128]{3,0,2,1:T(8,128)S(1)}, u32[]{:S(2)}, u32[]{:S(2)}) collective-permute-start(f32[32,4,1,128]{3,0,2,1:T(8,128)S(1)} %get-tuple-element.16), channel_id=1, source_target_pairs={{1,0},{2,1},{3,2},{0,3},{5,4},{6,5},{7,6},{4,7},{9,8},{10,9},{11,1... | collective-permute-start | bytes 196616 | tf_op jit(solution)/shard_map/ppermute | solution.py:18
  125.6 5.3 %collective-permute-start.7 = (f32[32,4,1,128]{3,0,2,1:T(8,128)S(1)}, f32[32,4,1,128]{3,0,2,1:T(8,128)S(1)}, u32[]{:S(2)}, u32[]{:S(2)}) collective-permute-start(f32[32,4,1,128]{3,0,2,1:T(8,128)S(1)} %get-tuple-element.17), channel_id=1, source_target_pairs={{0,1},{1,2},{2,3},{3,0},{4,5},{5,6},{6,7},{7,4},{8,9},{9,10},{10,1... | collective-permute-start | bytes 196616 | tf_op jit(solution)/shard_map/ppermute | solution.py:15
  184.4 6.8 %collective-permute-start.9 = (f32[32,1,16,128]{3,0,2,1:T(8,128)S(1)}, f32[32,1,16,128]{3,0,2,1:T(8,128)S(1)}, u32[]{:S(2)}, u32[]{:S(2)}) collective-permute-start(f32[32,1,16,128]{3,0,2,1:T(8,128)S(1)} %get-tuple-element.24), channel_id=1, source_target_pairs={{0,4},{4,8},{8,12},{12,16},{16,20},{20,24},{24,28},{28,0},{1,5},{5... | collective-permute-start | bytes 786440 | tf_op jit(solution)/shard_map/ppermute | solution.py:15
  184.4 6.8 %collective-permute-start.8 = (f32[32,1,16,128]{3,0,2,1:T(8,128)S(1)}, f32[32,1,16,128]{3,0,2,1:T(8,128)S(1)}, u32[]{:S(2)}, u32[]{:S(2)}) collective-permute-start(f32[32,1,16,128]{3,0,2,1:T(8,128)S(1)} %get-tuple-element.25), channel_id=1, source_target_pairs={{4,0},{8,4},{12,8},{16,12},{20,16},{24,20},{28,24},{0,28},{5,1},{9... | collective-permute-start | bytes 786440 | tf_op jit(solution)/shard_map/ppermute | solution.py:18
  191.2 4.3 %collective-permute-start.10 = (f32[32,4,1,128]{3,0,2,1:T(8,128)S(1)}, f32[32,4,1,128]{3,0,2,1:T(8,128)S(1)}, u32[]{:S(2)}, u32[]{:S(2)}) collective-permute-start(f32[32,4,1,128]{3,0,2,1:T(8,128)S(1)} %get-tuple-element.14), channel_id=1, source_target_pairs={{1,0},{2,1},{3,2},{0,3},{5,4},{6,5},{7,6},{4,7},{9,8},{10,9},{11,1... | collective-permute-start | bytes 196616 | tf_op jit(solution)/shard_map/ppermute | solution.py:18
  191.3 4.8 %collective-permute-start.11 = (f32[32,4,1,128]{3,0,2,1:T(8,128)S(1)}, f32[32,4,1,128]{3,0,2,1:T(8,128)S(1)}, u32[]{:S(2)}, u32[]{:S(2)}) collective-permute-start(f32[32,4,1,128]{3,0,2,1:T(8,128)S(1)} %get-tuple-element.15), channel_id=1, source_target_pairs={{0,1},{1,2},{2,3},{3,0},{4,5},{5,6},{6,7},{7,4},{8,9},{9,10},{10,1... | collective-permute-start | bytes 196616 | tf_op jit(solution)/shard_map/ppermute | solution.py:15
where the time goes:
time: 254 us
  blocking collectives  171 us (67%)
  other arithmetic  28.9 us (11%)
  waiting for transfers between devices  24.1 us (9%)
  matrix products  13.3 us (5%)
  starting transfers between devices  11.6 us (5%)
  local copies, waits for them, and re-layouts  3.44 us (1%)
    psum x3, blocking collectives, per_device(): lax.psum((inner_block(current, image), inner_block(image, image)), ('gx',...  131 us
    psum x1, blocking collectives, per_device(): probe_matrix = lax.psum(inner_block(probes, probes), ('gx', 'gy'))  40.3 us
    ppermute x6, waiting for transfers between devices, with_halo(): lax.ppermute(lax.slice_in_dim(block, block.shape[dim] - width, None, axis...  16.7 us
    another operation x12, other arithmetic, inverse_lower(): lower_factor = jnp.linalg.cholesky(gram_matrix)  14.4 us
    another operation x6, other arithmetic, inverse_lower(): lax.linalg.triangular_solve(lower_factor, identity_matrix, left_side=True...  11 us
    dot_general x9, matrix products, combine(): jnp.einsum('pxyz,pq->qxyz', vectors, matrix, precision=lax.Precision.HIGH...  7.62 us
    ppermute x6, waiting for transfers between devices, with_halo(): lax.ppermute(lax.slice_in_dim(block, 0, width, axis=dim), axis, backward)  7.37 us
    ppermute x6, starting transfers between devices, with_halo(): lax.ppermute(lax.slice_in_dim(block, 0, width, axis=dim), axis, backward)  5.89 us
  transfers between devices with their start and end apart: 12, of which 10 were waited for; matrix products, arithmetic and copies ran while one was open for 0% of the time, Pallas kernels for 0%

commit v1 on v0

--- a/solution.py
+++ b/solution.py
@@ -56,7 +56,7 @@
     )
     scale_factor = 1.0 / jnp.sqrt(jnp.float32(total_cells))
     probes = (2.0 * probe_signs.astype(jnp.float32) - 1.0) * scale_factor
-    probe_matrix = lax.psum(inner_block(probes, probes), ("gx", "gy"))
+    probe_matrix = jnp.sum(lax.all_gather(inner_block(probes, probes), ("gx", "gy")), axis=0)
     lower_factor, inverse = inverse_lower(probe_matrix)
     current = combine(probes, inverse.T)
     previous = None

time: 254 us -> 281 us (1.11)
  blocking collectives: 171 us -> 192 us
  starting transfers between devices: 11.6 us -> 14.7 us
    all_gather x0 -> x1, blocking collectives: none -> 61.2 us  [per_device(): lax.all_gather(inner_block(probes, probes), ('gx', 'gy'))]
    psum x1 -> x0, blocking collectives: 40.3 us -> none  [per_device(): probe_matrix = lax.psum(inner_block(probes, probes), ('gx', 'gy'))]
  transfers between devices with their start and end apart: 12 -> 12, of which waited for: 10 -> 11; matrix products, arithmetic and copies ran while one was open for 0% -> 0% of each run, Pallas kernels for 0% -> 0%
where the time goes in v1:
time: 281 us; the launch traced here: 280 us
  blocking collectives  192 us (68%)
  other arithmetic  29 us (10%)
  waiting for transfers between devices  26.7 us (10%)
  starting transfers between devices  14.7 us (5%)
  matrix products  13.3 us (5%)
  local copies, waits for them, and re-layouts  3.45 us (1%)
    psum x3, blocking collectives, per_device(): lax.psum((inner_block(current, image), inner_block(image, image)), ('gx',...  131 us
    all_gather x1, blocking collectives, per_device(): lax.all_gather(inner_block(probes, probes), ('gx', 'gy'))  61.2 us
    ppermute x6, waiting for transfers between devices, with_halo(): lax.ppermute(lax.slice_in_dim(block, block.shape[dim] - width, None, axis...  17 us
    another operation x12, other arithmetic, inverse_lower(): lower_factor = jnp.linalg.cholesky(gram_matrix)  14.4 us
    another operation x6, other arithmetic, inverse_lower(): lax.linalg.triangular_solve(lower_factor, identity_matrix, left_side=True...  11 us
    ppermute x6, waiting for transfers between devices, with_halo(): lax.ppermute(lax.slice_in_dim(block, 0, width, axis=dim), axis, backward)  9.69 us
    ppermute x6, starting transfers between devices, with_halo(): lax.ppermute(lax.slice_in_dim(block, 0, width, axis=dim), axis, backward)  8.46 us
    dot_general x9, matrix products, combine(): jnp.einsum('pxyz,pq->qxyz', vectors, matrix, precision=lax.Precision.HIGH...  7.62 us
  transfers between devices with their start and end apart: 12, of which 11 were waited for; matrix products, arithmetic and copies ran while one was open for 0% of the time, Pallas kernels for 0%

profile of v1, /device:TPU:14, one launch (start us, length us, event | category | flops | bytes accessed | tf_op | source)
XLA Modules:
  0.0 280.3 jit_solution(4371367451591645934)
XLA Ops:
  2.6 61.2 %all-gather = f32[1024,32]{1,0:T(8,128)S(1)} all-gather(f32[32,32]{1,0:T(8,128)S(1)} %convolution_bitcast_fusion.10), channel_id=2, replica_groups=mesh['gx'=8,'gy'=4] {'gx','gy'}, dimensions={0}, use_global_device_ids=true | all-gather | bytes 135168 | tf_op jit(solution)/shard_map/all_gather | solution.py:59
  64.0 2.9 %cholesky.74 = f32[32,32]{1,0:T(8,128)S(1)} custom-call(f32[32,32]{1,0:T(8,128)S(1)} %fusion.38), custom_call_target="Cholesky" | custom-call | tf_op jit(solution)/shard_map/jit(cholesky)/cholesky | solution.py:43
  68.2 2.4 custom-call.8
  71.8 2.3 collective-permute-start.1
  74.5 3.1 %collective-permute-done.1 = f32[32,1,16,128]{3,0,2,1:T(8,128)S(1)} collective-permute-done((f32[32,1,16,128]{3,0,2,1:T(8,128)S(1)}, f32[32,1,16,128]{3,0,2,1:T(8,128)S(1)}, u32[]{:S(2)}, u32[]{:S(2)}) %collective-permute-start.1) | collective-permute-done | bytes 262176 | tf_op jit(solution)/shard_map/ppermute | solution.py:15
  77.7 2.8 %collective-permute-done = f32[32,1,16,128]{3,0,2,1:T(8,128)S(1)} collective-permute-done((f32[32,1,16,128]{3,0,2,1:T(8,128)S(1)}, f32[32,1,16,128]{3,0,2,1:T(8,128)S(1)}, u32[]{:S(2)}, u32[]{:S(2)}) %collective-permute-start) | collective-permute-done | bytes 262176 | tf_op jit(solution)/shard_map/ppermute | solution.py:18
  80.5 4.7 %collective-permute-start.2 = (f32[32,4,1,128]{3,0,2,1:T(8,128)S(1)}, f32[32,4,1,128]{3,0,2,1:T(8,128)S(1)}, u32[]{:S(2)}, u32[]{:S(2)}) collective-permute-start(f32[32,4,1,128]{3,0,2,1:T(8,128)S(1)} %get-tuple-element.21), channel_id=1, source_target_pairs={{1,0},{2,1},{3,2},{0,3},{5,4},{6,5},{7,6},{4,7},{9,8},{10,9},{11,1... | collective-permute-start | bytes 196616 | tf_op jit(solution)/shard_map/ppermute | solution.py:18
  85.2 1.9 collective-permute-done.2
  87.1 3.4 %collective-permute-done.3 = f32[32,4,1,128]{3,0,2,1:T(8,128)S(1)} collective-permute-done((f32[32,4,1,128]{3,0,2,1:T(8,128)S(1)}, f32[32,4,1,128]{3,0,2,1:T(8,128)S(1)}, u32[]{:S(2)}, u32[]{:S(2)}) %collective-permute-start.3) | collective-permute-done | bytes 65568 | tf_op jit(solution)/shard_map/ppermute | solution.py:15
  92.0 43.7 %all-reduce.2 = (f32[32,32]{0,1:T(8,128)S(1)}, f32[32,32]{1,0:T(8,128)S(1)}) all-reduce(f32[32,32]{0,1:T(8,128)S(1)} %convolution_bitcast_fusion.7, f32[32,32]{1,0:T(8,128)S(1)} %convolution_bitcast_fusion.8), channel_id=1, replica_groups=mesh['gx'=8,'gy'=4] {'gx','gy'}, use_global_device_ids=true, to_apply=%region_4.7 | all-reduce | flops 2048 | bytes 16384 | tf_op jit(solution)/shard_map/psum | solution.py:70
  136.7 2.9 %cholesky.85 = f32[32,32]{1,0:T(8,128)S(1)} custom-call(f32[32,32]{1,0:T(8,128)S(1)} %fusion.36), custom_call_target="Cholesky" | custom-call | tf_op jit(solution)/shard_map/jit(cholesky)/cholesky | solution.py:43
  140.9 2.4 custom-call.9
  146.3 4.1 %collective-permute-done.5 = f32[32,1,16,128]{3,0,2,1:T(8,128)S(1)} collective-permute-done((f32[32,1,16,128]{3,0,2,1:T(8,128)S(1)}, f32[32,1,16,128]{3,0,2,1:T(8,128)S(1)}, u32[]{:S(2)}, u32[]{:S(2)}) %collective-permute-start.5) | collective-permute-done | bytes 262176 | tf_op jit(solution)/shard_map/ppermute | solution.py:15
  151.2 1.9 collective-permute-start.7
  153.3 2.0 collective-permute-done.6
  158.4 44.8 %all-reduce.1 = (f32[32,32]{0,1:T(8,128)S(1)}, f32[32,32]{1,0:T(8,128)S(1)}) all-reduce(f32[32,32]{0,1:T(8,128)S(1)} %convolution_bitcast_fusion.4, f32[32,32]{1,0:T(8,128)S(1)} %convolution_bitcast_fusion.5), channel_id=1, replica_groups=mesh['gx'=8,'gy'=4] {'gx','gy'}, use_global_device_ids=true, to_apply=%region_6.9 | all-reduce | flops 2048 | bytes 16384 | tf_op jit(solution)/shard_map/psum | solution.py:70
  204.2 2.9 %cholesky.96 = f32[32,32]{1,0:T(8,128)S(1)} custom-call(f32[32,32]{1,0:T(8,128)S(1)} %fusion.33), custom_call_target="Cholesky" | custom-call | tf_op jit(solution)/shard_map/jit(cholesky)/cholesky | solution.py:43
  208.4 2.4 custom-call.10
  213.7 5.4 %collective-permute-done.9 = f32[32,1,16,128]{3,0,2,1:T(8,128)S(1)} collective-permute-done((f32[32,1,16,128]{3,0,2,1:T(8,128)S(1)}, f32[32,1,16,128]{3,0,2,1:T(8,128)S(1)}, u32[]{:S(2)}, u32[]{:S(2)}) %collective-permute-start.9) | collective-permute-done | bytes 262176 | tf_op jit(solution)/shard_map/ppermute | solution.py:15
  219.2 2.0 collective-permute-start.11
  221.4 2.3 collective-permute-done.10
  227.0 42.4 %all-reduce = (f32[32,32]{1,0:T(8,128)S(1)}, f32[32,32]{0,1:T(8,128)S(1)}) all-reduce(f32[32,32]{1,0:T(8,128)S(1)} %convolution_bitcast_fusion.2, f32[32,32]{0,1:T(8,128)S(1)} %convolution_bitcast_fusion.1), channel_id=1, replica_groups=mesh['gx'=8,'gy'=4] {'gx','gy'}, use_global_device_ids=true, to_apply=%region_7.10 | all-reduce | flops 2048 | bytes 16384 | tf_op jit(solution)/shard_map/psum | solution.py:70
  270.4 2.9 %cholesky.107 = f32[32,32]{1,0:T(8,128)S(1)} custom-call(f32[32,32]{1,0:T(8,128)S(1)} %fusion.30), custom_call_target="Cholesky" | custom-call | tf_op jit(solution)/shard_map/jit(cholesky)/cholesky | solution.py:43
  274.6 2.4 custom-call.11
  (77 shorter events, 29.8 us)
Async XLA Ops:
  71.8 5.8 %collective-permute-start.1 = (f32[32,1,16,128]{3,0,2,1:T(8,128)S(1)}, f32[32,1,16,128]{3,0,2,1:T(8,128)S(1)}, u32[]{:S(2)}, u32[]{:S(2)}) collective-permute-start(f32[32,1,16,128]{3,0,2,1:T(8,128)S(1)} %get-tuple-element.39), channel_id=1, source_target_pairs={{0,4},{4,8},{8,12},{12,16},{16,20},{20,24},{24,28},{28,0},{1,5},{5... | collective-permute-start | bytes 786440 | tf_op jit(solution)/shard_map/ppermute | solution.py:15
  74.1 6.4 %collective-permute-start = (f32[32,1,16,128]{3,0,2,1:T(8,128)S(1)}, f32[32,1,16,128]{3,0,2,1:T(8,128)S(1)}, u32[]{:S(2)}, u32[]{:S(2)}) collective-permute-start(f32[32,1,16,128]{3,0,2,1:T(8,128)S(1)} %get-tuple-element.40), channel_id=1, source_target_pairs={{4,0},{8,4},{12,8},{16,12},{20,16},{24,20},{28,24},{0,28},{5,1},{9... | collective-permute-start | bytes 786440 | tf_op jit(solution)/shard_map/ppermute | solution.py:18
  74.5 10.7 %copy-start = (f32[2,16,128]{2,1,0:T(8,128)S(1)}, f32[2,16,128]{2,1,0:T(8,128)}, u32[]{:S(2)}) copy-start(f32[2,16,128]{2,1,0:T(8,128)} %param.6) | copy-start | bytes 49156
  80.5 6.6 %collective-permute-start.2 = (f32[32,4,1,128]{3,0,2,1:T(8,128)S(1)}, f32[32,4,1,128]{3,0,2,1:T(8,128)S(1)}, u32[]{:S(2)}, u32[]{:S(2)}) collective-permute-start(f32[32,4,1,128]{3,0,2,1:T(8,128)S(1)} %get-tuple-element.21), channel_id=1, source_target_pairs={{1,0},{2,1},{3,2},{0,3},{5,4},{6,5},{7,6},{4,7},{9,8},{10,9},{11,1... | collective-permute-start | bytes 196616 | tf_op jit(solution)/shard_map/ppermute | solution.py:18
  85.2 5.3 %collective-permute-start.3 = (f32[32,4,1,128]{3,0,2,1:T(8,128)S(1)}, f32[32,4,1,128]{3,0,2,1:T(8,128)S(1)}, u32[]{:S(2)}, u32[]{:S(2)}) collective-permute-start(f32[32,4,1,128]{3,0,2,1:T(8,128)S(1)} %get-tuple-element.22), channel_id=1, source_target_pairs={{0,1},{1,2},{2,3},{3,0},{4,5},{5,6},{6,7},{7,4},{8,9},{9,10},{10,1... | collective-permute-start | bytes 196616 | tf_op jit(solution)/shard_map/ppermute | solution.py:15
  144.3 6.1 %collective-permute-start.5 = (f32[32,1,16,128]{3,0,2,1:T(8,128)S(1)}, f32[32,1,16,128]{3,0,2,1:T(8,128)S(1)}, u32[]{:S(2)}, u32[]{:S(2)}) collective-permute-start(f32[32,1,16,128]{3,0,2,1:T(8,128)S(1)} %get-tuple-element.33), channel_id=1, source_target_pairs={{0,4},{4,8},{8,12},{12,16},{16,20},{20,24},{24,28},{28,0},{1,5},{5... | collective-permute-start | bytes 786440 | tf_op jit(solution)/shard_map/ppermute | solution.py:15
  144.3 6.7 %collective-permute-start.4 = (f32[32,1,16,128]{3,0,2,1:T(8,128)S(1)}, f32[32,1,16,128]{3,0,2,1:T(8,128)S(1)}, u32[]{:S(2)}, u32[]{:S(2)}) collective-permute-start(f32[32,1,16,128]{3,0,2,1:T(8,128)S(1)} %get-tuple-element.34), channel_id=1, source_target_pairs={{4,0},{8,4},{12,8},{16,12},{20,16},{24,20},{28,24},{0,28},{5,1},{9... | collective-permute-start | bytes 786440 | tf_op jit(solution)/shard_map/ppermute | solution.py:18
  151.0 4.3 %collective-permute-start.6 = (f32[32,4,1,128]{3,0,2,1:T(8,128)S(1)}, f32[32,4,1,128]{3,0,2,1:T(8,128)S(1)}, u32[]{:S(2)}, u32[]{:S(2)}) collective-permute-start(f32[32,4,1,128]{3,0,2,1:T(8,128)S(1)} %get-tuple-element.19), channel_id=1, source_target_pairs={{1,0},{2,1},{3,2},{0,3},{5,4},{6,5},{7,6},{4,7},{9,8},{10,9},{11,1... | collective-permute-start | bytes 196616 | tf_op jit(solution)/shard_map/ppermute | solution.py:18
  151.2 4.5 %collective-permute-start.7 = (f32[32,4,1,128]{3,0,2,1:T(8,128)S(1)}, f32[32,4,1,128]{3,0,2,1:T(8,128)S(1)}, u32[]{:S(2)}, u32[]{:S(2)}) collective-permute-start(f32[32,4,1,128]{3,0,2,1:T(8,128)S(1)} %get-tuple-element.20), channel_id=1, source_target_pairs={{0,1},{1,2},{2,3},{3,0},{4,5},{5,6},{6,7},{7,4},{8,9},{9,10},{10,1... | collective-permute-start | bytes 196616 | tf_op jit(solution)/shard_map/ppermute | solution.py:15
  211.7 7.4 %collective-permute-start.9 = (f32[32,1,16,128]{3,0,2,1:T(8,128)S(1)}, f32[32,1,16,128]{3,0,2,1:T(8,128)S(1)}, u32[]{:S(2)}, u32[]{:S(2)}) collective-permute-start(f32[32,1,16,128]{3,0,2,1:T(8,128)S(1)} %get-tuple-element.27), channel_id=1, source_target_pairs={{0,4},{4,8},{8,12},{12,16},{16,20},{20,24},{24,28},{28,0},{1,5},{5... | collective-permute-start | bytes 786440 | tf_op jit(solution)/shard_map/ppermute | solution.py:15
  211.8 7.3 %collective-permute-start.8 = (f32[32,1,16,128]{3,0,2,1:T(8,128)S(1)}, f32[32,1,16,128]{3,0,2,1:T(8,128)S(1)}, u32[]{:S(2)}, u32[]{:S(2)}) collective-permute-start(f32[32,1,16,128]{3,0,2,1:T(8,128)S(1)} %get-tuple-element.28), channel_id=1, source_target_pairs={{4,0},{8,4},{12,8},{16,12},{20,16},{24,20},{28,24},{0,28},{5,1},{9... | collective-permute-start | bytes 786440 | tf_op jit(solution)/shard_map/ppermute | solution.py:18
  219.1 4.6 %collective-permute-start.10 = (f32[32,4,1,128]{3,0,2,1:T(8,128)S(1)}, f32[32,4,1,128]{3,0,2,1:T(8,128)S(1)}, u32[]{:S(2)}, u32[]{:S(2)}) collective-permute-start(f32[32,4,1,128]{3,0,2,1:T(8,128)S(1)} %get-tuple-element.17), channel_id=1, source_target_pairs={{1,0},{2,1},{3,2},{0,3},{5,4},{6,5},{7,6},{4,7},{9,8},{10,9},{11,1... | collective-permute-start | bytes 196616 | tf_op jit(solution)/shard_map/ppermute | solution.py:18
  219.2 5.1 %collective-permute-start.11 = (f32[32,4,1,128]{3,0,2,1:T(8,128)S(1)}, f32[32,4,1,128]{3,0,2,1:T(8,128)S(1)}, u32[]{:S(2)}, u32[]{:S(2)}) collective-permute-start(f32[32,4,1,128]{3,0,2,1:T(8,128)S(1)} %get-tuple-element.18), channel_id=1, source_target_pairs={{0,1},{1,2},{2,3},{3,0},{4,5},{5,6},{6,7},{7,4},{8,9},{9,10},{10,1... | collective-permute-start | bytes 196616 | tf_op jit(solution)/shard_map/ppermute | solution.py:15
